TPU v7x, 32 devices: a whole 2x2x4 slice. The times are simulated.
32 devices in a mesh: groups: 2 (over y), row: 4 (over z), col: 4 (over x, core).
Axes of the slice: x: 2, y: 2, z: 4, core: 2. Of those that a mesh axis runs over, the one named last changes fastest.
Arguments:
- tokens: bfloat16 [128, 8192], P(('groups', 'row'), 'col'), parts along dimension 0, may hold values from -6 to 6
- gate_tiles: bfloat16 [256, 4, 12, 128, 256], P(('groups', 'row'), 'col'), parts along dimension 0, may hold values from -0.09375 to 0.09375
- gate_lists: int32 [256, 4, 12], P(('groups', 'row'), 'col'), parts along dimension 0, may hold values from 0 to 15, as said below
- gate_counts: int32 [256, 4], P(('groups', 'row'), 'col'), parts along dimension 0, may hold values from 4 to 12, as said below
- down_tiles: bfloat16 [128, 4, 24, 128, 128], P(('groups', 'row'), 'col'), parts along dimension 0, may hold values from -0.0625 to 0.0625
- down_lists: int32 [128, 4, 24], P(('groups', 'row'), 'col'), parts along dimension 0, may hold values from 0 to 31, as said below
- down_counts: int32 [128, 4], P(('groups', 'row'), 'col'), parts along dimension 0, may hold values from 8 to 24, as said below
Outputs:
- ffn_out: bfloat16 [128, 8192], P(('groups', 'col'), 'row'), parts along dimension 0
There are 2 independent parts, one for each index of `groups`. A program takes and returns all parts, laid end to end along the dimension named above; each array names one. Nothing has to cross between parts.
Inputs may be any that keep to these rules, and one draw needn't show every extreme that they name: `gate_lists`: within each panel the 12 entries are distinct; only the first gate_counts entries are used. `gate_counts`: some panel uses all 12 slots. `down_lists`: within each panel the 24 entries are distinct; only the first down_counts entries are used. `down_counts`: some panel uses all 24 slots.
All inputs are finite; a program needn't handle non-finite values.
Results may differ from a plain program's by a relative error of at most 0.005.
Values may be sent and summed in bfloat16 or wider, within the bound.
No kernel may reach another device: no remote copies, remote signals or barrier semaphores. Data moves between devices by JAX's collectives and lax.ppermute only.
A program may use at most 192 MiB of HBM per device.

v0:
```python
import jax
import jax.numpy as jnp
from jax import lax
from jax.sharding import PartitionSpec as P


def slot_mask(slot_counts, slot_total):
    slots = jnp.arange(slot_total, dtype=jnp.int32)
    return (slots < slot_counts[..., None]).astype(jnp.bfloat16)


def local(tokens, gate_tiles, gate_lists, gate_counts, down_tiles, down_lists, down_counts):
    block = gate_tiles.shape[3]
    columns = lax.axis_size("col")
    local_hidden = gate_tiles.shape[0]
    all_tokens = lax.all_gather(tokens, "row", axis=0, tiled=True)
    total_rows = all_tokens.shape[0]
    quarter = total_rows // columns
    lists_here = gate_lists[:, 0, :]
    keep_gate = slot_mask(gate_counts[:, 0], gate_lists.shape[2])
    tiles_here = gate_tiles[:, 0]
    row_count = all_tokens.shape[0]
    blocks_grid = all_tokens.reshape(row_count, -1, block)
    chosen = blocks_grid[:, lists_here, :] * keep_gate[None, :, :, None]
    product = jnp.einsum("rhsk,hskc->rhc", chosen, tiles_here, preferred_element_type=jnp.float32)
    summed = lax.psum(product.reshape(row_count, -1), "col")
    own_rows = lax.dynamic_slice_in_dim(summed, lax.axis_index("col") * quarter, quarter, 0)
    paired = own_rows.reshape(quarter, local_hidden, 2, block)
    hidden = (
        (jax.nn.silu(paired[:, :, 0]) * paired[:, :, 1]).astype(jnp.bfloat16).reshape(quarter, -1)
    )
    hidden_all = lax.all_gather(hidden, "row", axis=1, tiled=True)
    hidden_width = hidden_all.shape[1]
    quarter_blocks = hidden_width // (block * columns)
    tiles_all = lax.all_gather(down_tiles, "col", axis=1, tiled=True)
    lists_all, counts_all = (
        lax.all_gather(down_lists, "col", axis=1, tiled=True),
        lax.all_gather(down_counts, "col", axis=1, tiled=True),
    )
    offsets = (jnp.arange(columns, dtype=jnp.int32) * quarter_blocks)[None, :, None]
    block_index = lists_all + offsets
    keep_down = slot_mask(counts_all, lists_all.shape[2])
    blocks_grid = hidden_all.reshape(quarter, -1, block)
    chosen = blocks_grid[:, block_index, :] * keep_down[None, :, :, :, None]
    product = jnp.einsum("tdqsk,dqskc->tdc", chosen, tiles_all, preferred_element_type=jnp.float32)
    result = product.reshape(quarter, -1)
    return result.astype(jnp.bfloat16)


def solution(mesh):
    return jax.shard_map(
        local,
        mesh=mesh,
        in_specs=(
            P(("groups", "row"), "col"),
            P(("groups", "row"), "col", None, None, None),
            P(("groups", "row"), "col", None),
            P(("groups", "row"), "col"),
            P(("groups", "row"), "col", None, None, None),
            P(("groups", "row"), "col", None),
            P(("groups", "row"), "col"),
        ),
        out_specs=P(("groups", "col"), "row"),
        check_vma=False,
    )
```

profile of v0, /device:TPU:0, one launch (start us, length us, event | category | flops | bytes accessed | tf_op | source)
XLA Modules:
  0.0 430.9 jit_solution(15397803045704059399)
XLA Ops:
  6.5 0.0 all-reduce.2.cloned.1.call-start
  6.5 15.8 %all_gather.15 = bf16[64,2048]{1,0:T(8,128)(2,1)S(1)} all-gather(bf16[16,2048]{1,0:T(8,128)(2,1)} %param.7), channel_id=1, replica_groups=mesh['groups'=2,'row'=4,'col'=4] {'row'}, dimensions={0}, use_global_device_ids=true | all-gather | bytes 327680 | tf_op jit(solution)/shard_map/all_gather | solution.py:16
  22.4 0.1 copy_bitcast_fusion.1
  22.4 0.7 compare_select_fusion.1
  23.1 0.1 copy.36
  23.2 0.1 reshape.84
  23.3 0.7 fusion.27
  24.1 13.3 %gather_fusion = bf16[384,64,128]{2,1,0:T(8,128)(2,1)} fusion(bf16[64,16,128]{2,0,1:T(8,128)(2,1)S(1)} %copy_bitcast_fusion.1, s32[1024]{0:T(1024)S(1)} %pad_clamp_fusion.1), kind=kCustom, calls=%fused_computation | custom fusion | bytes 12584448 | tf_op jit(solution)/shard_map/gather | solution.py:24
  37.4 12.6 %fusion.8 = f32[32,8,8,256]{3,2,1,0:T(8,128)S(1)} fusion(bf16[32,1,12,128,256]{4,3,2,1,0:T(8,128)(2,1)} %param.8, bf16[32,12,64,128]{3,2,1,0:T(8,128)(2,1)} %bitcast.83, bf16[32,12]{1,0:T(8,128)(2,1)S(1)} %fusion.27), kind=kOutput, calls=%fused_computation.11 | convolution fusion | flops 1613758464 | bytes 33555200 | tf_op jit(solution)/shard_map/rhsk,hskc->rhc/dot_general | solution.py:25
  50.0 1.5 copy.49
  51.5 0.0 all-reduce.2.cloned.1.call-update
  51.6 0.0 all-gather.3.cloned.1.call-start
  51.6 0.0 copy-start
  51.6 0.0 copy-start.1
  51.6 0.7 all-gather.3.cloned.1.call-update
  52.3 0.0 copy-done
  52.3 5.2 %all_gather.17 = s32[16,4,24]{2,0,1:T(8,128)S(1)} all-gather(s32[16,1,24]{2,0,1:T(8,128)S(1)} %bitcast.89), channel_id=1, replica_groups=mesh['groups'=2,'row'=4,'col'=4] {'col'}, dimensions={1}, use_global_device_ids=true | all-gather | bytes 7680 | tf_op jit(solution)/shard_map/all_gather | solution.py:37
  57.5 0.1 compare_select_fusion
  57.6 0.1 reshape.92
  57.7 0.0 copy-done.1
  57.7 5.0 %all-gather = s32[4,1,16]{2,1,0:T(1,128)S(1)} all-gather(s32[1,1,16]{2,1,0:T(1,128)S(1)} %bitcast.92), channel_id=1, replica_groups=mesh['groups'=2,'row'=4,'col'=4] {'col'}, dimensions={0}, use_global_device_ids=true | all-gather | bytes 320 | tf_op jit(solution)/shard_map/all_gather | solution.py:38
  62.8 0.1 fusion.26
  62.9 41.8 %all-reduce.2.cloned.1.call-done = f32[64,8192]{1,0:T(8,128)} async-done(((f32[64,8192]{1,0:T(8,128)}), f32[64,8192]{1,0:T(8,128)}) %all-reduce.2.cloned.1.call-update) | async-done | bytes 2097168 | tf_op jit(solution)/shard_map/psum | solution.py:26
  104.7 1.1 constant_dynamic-slice_fusion
  105.7 0.4 reshape.80
  106.2 1.3 slice_reduce_fusion.1
  107.5 0.3 fusion.22
  107.9 15.7 %all_gather.16 = bf16[16,16384]{1,0:T(8,128)(2,1)S(1)} all-gather(bf16[16,4096]{1,0:T(8,128)(2,1)S(1)} %fusion.22), channel_id=1, replica_groups=mesh['groups'=2,'row'=4,'col'=4] {'row'}, dimensions={1}, use_global_device_ids=true | all-gather | bytes 655360 | tf_op jit(solution)/shard_map/all_gather | solution.py:32
  123.5 0.1 copy_bitcast_fusion
  123.6 5.7 %gather_fusion.1 = bf16[1536,16,128]{2,1,0:T(8,128)(2,1)} fusion(bf16[16,128,128]{2,0,1:T(8,128)(2,1)S(1)} %copy_bitcast_fusion, s32[2048]{0:T(1024)S(1)} %pad_clamp_fusion), kind=kCustom, calls=%fused_computation.1 | custom fusion | bytes 12589056 | tf_op jit(solution)/shard_map/gather | solution.py:44
  129.3 274.2 %all-gather.3.cloned.1.call-done = bf16[16,4,24,128,128]{4,3,2,0,1:T(8,128)(2,1)} async-done(((bf16[16,1,24,128,128]{4,3,2,0,1:T(8,128)(2,1)}), bf16[16,4,24,128,128]{4,3,2,0,1:T(8,128)(2,1)}) %all-gather.3.cloned.1.call-update) | async-done | bytes 50331664 | tf_op jit(solution)/shard_map/all_gather | solution.py:35
  403.5 19.9 %fusion.19 = bf16[16,2,8,128]{3,2,1,0:T(8,128)(2,1)S(1)} fusion(bf16[16,4,24,128,128]{4,3,2,0,1:T(8,128)(2,1)} %all-gather.3.cloned.1.call-done, bf16[16,4,24,16,128]{4,3,2,1,0:T(8,128)(2,1)} %bitcast.84, bf16[16,4,24]{2,0,1:T(8,128)(2,1)S(1)} %fusion.26), kind=kOutput, calls=%fused_computation.14 | convolution fusion | flops 808484864 | bytes 56691712 | tf_op jit(solution)/shard_map/tdqsk,dqskc->tdc/dot_general | solution.py:45
  423.5 0.6 copy.68
  (4 shorter events, 0.0 us)
Async XLA Ops:
  6.5 98.1 %all-reduce.2.cloned.1.call-start = ((), (), s32[]{:S(2)}) async-start(), calls=%async_computation | async-start | bytes 4194304 | tf_op jit(solution)/shard_map/psum | solution.py:26
  51.6 352.0 %all-gather.3.cloned.1.call-start = ((), (), s32[]{:S(2)}) async-start(), calls=%async_computation.1 | async-start | bytes 62914560 | tf_op jit(solution)/shard_map/all_gather | solution.py:35
  51.6 0.7 copy-start
  51.6 6.1 %copy-start.1 = (s32[16,1]{0,1:T(1,128)S(1)}, s32[16,1]{0,1:T(1,128)}, u32[]{:S(2)}) copy-start(s32[16,1]{0,1:T(1,128)} %param.13) | copy-start | bytes 196
Sparse Core Ops, SparseCore 0:
  51.7 52.9 all-reduce.1
  106.3 297.1 all-gather.2
where the time goes:
time: 431 us
  waiting for transfers between devices  317 us (74%)
  blocking collectives  41.7 us (10%)
  matrix products  32.5 us (8%)
  local copies, waits for them, and re-layouts  24.5 us (6%)
  between operations  13.5 us (3%)
    all_gather x1, waiting for transfers between devices, local(): tiles_all = lax.all_gather(down_tiles, 'col', axis=1, tiled=True)  274 us
    psum x1, waiting for transfers between devices, local(): summed = lax.psum(product.reshape(row_count, -1), 'col')  41.8 us
    dot_general x1, matrix products, local(): jnp.einsum('tdqsk,dqskc->tdc', chosen, tiles_all, preferred_element_type=...  19.9 us
    all_gather x1, blocking collectives, local(): all_tokens = lax.all_gather(tokens, 'row', axis=0, tiled=True)  15.8 us
    all_gather x1, blocking collectives, local(): hidden_all = lax.all_gather(hidden, 'row', axis=1, tiled=True)  15.7 us
    gather x1, local copies, waits for them, and re-layouts, local(): chosen = blocks_grid[:, lists_here, :] * keep_gate[None, :, :, None]  13.3 us
    dot_general x1, matrix products, local(): jnp.einsum('rhsk,hskc->rhc', chosen, tiles_here, preferred_element_type=j...  12.6 us
  transfers between devices with their start and end apart: 2, of which 2 were waited for; matrix products, arithmetic and copies ran while one was open for 2% of the time, Pallas kernels for 0%

commit v1 on v0

--- a/solution.py
+++ b/solution.py
@@ -2,6 +2,21 @@
 import jax.numpy as jnp
 from jax import lax
 from jax.sharding import PartitionSpec as P
+
+
+def deliver_teams(content):
+    extent = lax.axis_size("row")
+    item_now = sorted(((c, (c + 1) % extent) for c in range(extent)))
+    f_next = content
+    shelf = [f_next]
+    i = 1
+    while i < extent:
+        f_next = lax.ppermute(f_next, "row", item_now)
+        shelf.insert(0, f_next)
+        i += 1
+    now = jnp.concatenate(shelf, axis=0)
+    x_new = lax.axis_index("row") + 1
+    return jnp.roll(now, x_new * content.shape[0], axis=0)
 
 
 def slot_mask(slot_counts, slot_total):
@@ -13,7 +28,7 @@
     block = gate_tiles.shape[3]
     columns = lax.axis_size("col")
     local_hidden = gate_tiles.shape[0]
-    all_tokens = lax.all_gather(tokens, "row", axis=0, tiled=True)
+    all_tokens = deliver_teams(tokens)
     total_rows = all_tokens.shape[0]
     quarter = total_rows // columns
     lists_here = gate_lists[:, 0, :]

time: 431 us -> 432 us (level)
  blocking collectives: 41.7 us -> 25.9 us
  waiting for transfers between devices: 317 us -> 329 us
    all_gather x1 -> x0, blocking collectives: 15.8 us -> none  [local(): all_tokens = lax.all_gather(tokens, 'row', axis=0, tiled=True)]
    ppermute x0 -> x3, waiting for transfers between devices: none -> 15 us  [deliver_teams(): f_next = lax.ppermute(f_next, 'row', item_now)]
  transfers between devices with their start and end apart: 2 -> 5, of which waited for: 2 -> 5; matrix products, arithmetic and copies ran while one was open for 2% -> 3% of each run, Pallas kernels for 0% -> 0%
where the time goes in v1:
time: 432 us
  waiting for transfers between devices  329 us (76%)
  matrix products  32.5 us (8%)
  local copies, waits for them, and re-layouts  26.2 us (6%)
  blocking collectives  25.9 us (6%)
  between operations  13.6 us (3%)
    all_gather x1, waiting for transfers between devices, local(): tiles_all = lax.all_gather(down_tiles, 'col', axis=1, tiled=True)  274 us
    psum x1, waiting for transfers between devices, local(): summed = lax.psum(product.reshape(row_count, -1), 'col')  38.7 us
    dot_general x1, matrix products, local(): jnp.einsum('tdqsk,dqskc->tdc', chosen, tiles_all, preferred_element_type=...  19.9 us
    all_gather x1, blocking collectives, local(): hidden_all = lax.all_gather(hidden, 'row', axis=1, tiled=True)  15.7 us
    ppermute x3, waiting for transfers between devices, deliver_teams(): f_next = lax.ppermute(f_next, 'row', item_now)  15 us
    gather x1, local copies, waits for them, and re-layouts, local(): chosen = blocks_grid[:, lists_here, :] * keep_gate[None, :, :, None]  13.3 us
    dot_general x1, matrix products, local(): jnp.einsum('rhsk,hskc->rhc', chosen, tiles_here, preferred_element_type=j...  12.6 us
  transfers between devices with their start and end apart: 5, of which 5 were waited for; matrix products, arithmetic and copies ran while one was open for 3% of the time, Pallas kernels for 0%

profile of v1, /device:TPU:0, one launch (start us, length us, event | category | flops | bytes accessed | tf_op | source)
XLA Modules:
  0.0 431.8 jit_solution(2324533306513782068)
XLA Ops:
  6.5 0.0 all-reduce.2.cloned.1.call-start
  6.5 3.0 collective-permute-start
  9.6 0.7 compare_select_fusion.1
  10.3 3.8 collective-permute-done
  14.0 0.0 collective-permute-start.1
  14.0 0.7 fusion.27
  14.8 0.1 copy.35
  14.9 0.1 reshape.84
  15.0 5.1 %collective-permute-done.1 = bf16[16,2048]{1,0:T(8,128)(2,1)S(1)} collective-permute-done((bf16[16,2048]{1,0:T(8,128)(2,1)S(1)}, bf16[16,2048]{1,0:T(8,128)(2,1)S(1)}, u32[]{:S(2)}, u32[]{:S(2)}) %collective-permute-start.1) | collective-permute-done | bytes 65568 | tf_op jit(solution)/shard_map/ppermute | solution.py:14
  20.1 0.0 collective-permute-start.2
  20.1 6.1 %collective-permute-done.2 = bf16[16,2048]{1,0:T(8,128)(2,1)S(1)} collective-permute-done((bf16[16,2048]{1,0:T(8,128)(2,1)S(1)}, bf16[16,2048]{1,0:T(8,128)(2,1)S(1)}, u32[]{:S(2)}, u32[]{:S(2)}) %collective-permute-start.2) | collective-permute-done | bytes 65568 | tf_op jit(solution)/shard_map/ppermute | solution.py:14
  26.2 0.8 constant_dynamic-update-slice_fusion.4
  27.1 0.8 constant_dynamic-update-slice_fusion
  27.9 0.1 copy_bitcast_fusion.1
  28.0 13.3 %gather_fusion = bf16[384,64,128]{2,1,0:T(8,128)(2,1)} fusion(bf16[64,16,128]{2,0,1:T(8,128)(2,1)S(1)} %copy_bitcast_fusion.1, s32[1024]{0:T(1024)S(1)} %pad_clamp_fusion.1), kind=kCustom, calls=%fused_computation | custom fusion | bytes 12584448 | tf_op jit(solution)/shard_map/gather | solution.py:39
  41.3 12.6 %fusion.8 = f32[32,8,8,256]{3,2,1,0:T(8,128)S(1)} fusion(bf16[32,1,12,128,256]{4,3,2,1,0:T(8,128)(2,1)} %param.8, bf16[32,12,64,128]{3,2,1,0:T(8,128)(2,1)} %bitcast.83, bf16[32,12]{1,0:T(8,128)(2,1)S(1)} %fusion.27), kind=kOutput, calls=%fused_computation.11 | convolution fusion | flops 1613758464 | bytes 33555200 | tf_op jit(solution)/shard_map/rhsk,hskc->rhc/dot_general | solution.py:40
  53.9 1.5 copy.48
  55.5 0.0 all-reduce.2.cloned.1.call-update
  55.5 0.0 all-gather.3.cloned.1.call-start
  55.5 0.0 copy-start
  55.6 0.0 copy-start.1
  55.6 0.7 all-gather.3.cloned.1.call-update
  56.3 0.0 copy-done
  56.3 5.2 %all_gather.13 = s32[16,4,24]{2,0,1:T(8,128)S(1)} all-gather(s32[16,1,24]{2,0,1:T(8,128)S(1)} %bitcast.89), channel_id=1, replica_groups=mesh['groups'=2,'row'=4,'col'=4] {'col'}, dimensions={1}, use_global_device_ids=true | all-gather | bytes 7680 | tf_op jit(solution)/shard_map/all_gather | solution.py:52
  61.5 0.1 compare_select_fusion
  61.6 0.1 reshape.92
  61.7 0.0 copy-done.1
  61.7 5.0 %all-gather = s32[4,1,16]{2,1,0:T(1,128)S(1)} all-gather(s32[1,1,16]{2,1,0:T(1,128)S(1)} %bitcast.92), channel_id=1, replica_groups=mesh['groups'=2,'row'=4,'col'=4] {'col'}, dimensions={0}, use_global_device_ids=true | all-gather | bytes 320 | tf_op jit(solution)/shard_map/all_gather | solution.py:53
  66.7 0.1 fusion.26
  66.8 38.7 %all-reduce.2.cloned.1.call-done = f32[64,8192]{1,0:T(8,128)} async-done(((f32[64,8192]{1,0:T(8,128)}), f32[64,8192]{1,0:T(8,128)}) %all-reduce.2.cloned.1.call-update) | async-done | bytes 2097168 | tf_op jit(solution)/shard_map/psum | solution.py:41
  105.5 1.1 constant_dynamic-slice_fusion
  106.5 0.4 reshape.80
  107.0 1.3 slice_reduce_fusion.1
  108.3 0.3 fusion.22
  108.7 15.7 %all_gather.12 = bf16[16,16384]{1,0:T(8,128)(2,1)S(1)} all-gather(bf16[16,4096]{1,0:T(8,128)(2,1)S(1)} %fusion.22), channel_id=1, replica_groups=mesh['groups'=2,'row'=4,'col'=4] {'row'}, dimensions={1}, use_global_device_ids=true | all-gather | bytes 655360 | tf_op jit(solution)/shard_map/all_gather | solution.py:47
  124.3 0.1 copy_bitcast_fusion
  124.4 5.7 %gather_fusion.1 = bf16[1536,16,128]{2,1,0:T(8,128)(2,1)} fusion(bf16[16,128,128]{2,0,1:T(8,128)(2,1)S(1)} %copy_bitcast_fusion, s32[2048]{0:T(1024)S(1)} %pad_clamp_fusion), kind=kCustom, calls=%fused_computation.1 | custom fusion | bytes 12589056 | tf_op jit(solution)/shard_map/gather | solution.py:59
  130.1 274.2 %all-gather.3.cloned.1.call-done = bf16[16,4,24,128,128]{4,3,2,0,1:T(8,128)(2,1)} async-done(((bf16[16,1,24,128,128]{4,3,2,0,1:T(8,128)(2,1)}), bf16[16,4,24,128,128]{4,3,2,0,1:T(8,128)(2,1)}) %all-gather.3.cloned.1.call-update) | async-done | bytes 50331664 | tf_op jit(solution)/shard_map/all_gather | solution.py:50
  404.4 19.9 %fusion.19 = bf16[16,2,8,128]{3,2,1,0:T(8,128)(2,1)S(1)} fusion(bf16[16,4,24,128,128]{4,3,2,0,1:T(8,128)(2,1)} %all-gather.3.cloned.1.call-done, bf16[16,4,24,16,128]{4,3,2,1,0:T(8,128)(2,1)} %bitcast.84, bf16[16,4,24]{2,0,1:T(8,128)(2,1)S(1)} %fusion.26), kind=kOutput, calls=%fused_computation.14 | convolution fusion | flops 808484864 | bytes 56691712 | tf_op jit(solution)/shard_map/tdqsk,dqskc->tdc/dot_general | solution.py:60
  424.3 0.6 copy.67
  (10 shorter events, 0.1 us)
Async XLA Ops:
  6.5 98.9 %all-reduce.2.cloned.1.call-start = ((), (), s32[]{:S(2)}) async-start(), calls=%async_computation | async-start | bytes 4194304 | tf_op jit(solution)/shard_map/psum | solution.py:41
  6.5 7.5 %collective-permute-start = (bf16[16,2048]{1,0:T(8,128)(2,1)}, bf16[16,2048]{1,0:T(8,128)(2,1)S(1)}, u32[]{:S(2)}, u32[]{:S(2)}) collective-permute-start(bf16[16,2048]{1,0:T(8,128)(2,1)} %param.7), channel_id=1, source_target_pairs={{0,4},{4,8},{8,12},{12,0},{1,5},{5,9},{9,13},{13,1},{2,6},{6,10},{... | collective-permute-start | bytes 196616 | tf_op jit(solution)/shard_map/ppermute | solution.py:14
  14.0 6.1 %collective-permute-start.1 = (bf16[16,2048]{1,0:T(8,128)(2,1)S(1)}, bf16[16,2048]{1,0:T(8,128)(2,1)S(1)}, u32[]{:S(2)}, u32[]{:S(2)}) collective-permute-start(bf16[16,2048]{1,0:T(8,128)(2,1)S(1)} %collective-permute-done), channel_id=1, source_target_pairs={{0,4},{4,8},{8,12},{12,0},{1,5},{5,9},{9,13},{13,1},{2,6},{6,10},{... | collective-permute-start | bytes 196616 | tf_op jit(solution)/shard_map/ppermute | solution.py:14
  20.1 6.1 %collective-permute-start.2 = (bf16[16,2048]{1,0:T(8,128)(2,1)S(1)}, bf16[16,2048]{1,0:T(8,128)(2,1)S(1)}, u32[]{:S(2)}, u32[]{:S(2)}) collective-permute-start(bf16[16,2048]{1,0:T(8,128)(2,1)S(1)} %collective-permute-done.1), channel_id=1, source_target_pairs={{0,4},{4,8},{8,12},{12,0},{1,5},{5,9},{9,13},{13,1},{2,6},{6,10},{... | collective-permute-start | bytes 196616 | tf_op jit(solution)/shard_map/ppermute | solution.py:14
  55.5 348.9 %all-gather.3.cloned.1.call-start = ((), (), s32[]{:S(2)}) async-start(), calls=%async_computation.1 | async-start | bytes 62914560 | tf_op jit(solution)/shard_map/all_gather | solution.py:50
  55.5 0.7 copy-start
  55.6 6.1 %copy-start.1 = (s32[16,1]{0,1:T(1,128)S(1)}, s32[16,1]{0,1:T(1,128)}, u32[]{:S(2)}) copy-start(s32[16,1]{0,1:T(1,128)} %param.13) | copy-start | bytes 196
Sparse Core Ops, SparseCore 0:
  55.6 49.8 all-reduce.1
  107.1 297.1 all-gather.2
